TPU v7x, 32 devices: a whole 2x2x4 slice. The times are simulated.
32 devices in a mesh: col: 8 (over z, x), row: 4 (over y, core).
Axes of the slice: x: 2, y: 2, z: 4, core: 2. Of those that a mesh axis runs over, the one named last changes fastest.
Arguments:
- loads: float32 [4, 16, 2, 16, 128], P('row', 'col'), may hold values from -100 to 100
- stiffness: float32 [4, 32, 128], P('row', 'col'), may hold values from 0.5 to 2
- tile_info: int32 [4, 32, 4], P('row', 'col'), may hold values from 0 to 15, as said below
- offsets: int32 [4, 32, 2, 128], P('row', 'col'), may hold values from 0 to 127
Outputs:
- forces: float32 [4, 32, 16, 128], P('row', 'col')
- residual: float32 [4, 16, 2, 16, 128], P('row', 'col')
Inputs may be any that keep to these rules, and one draw needn't show every extreme that they name: tile_info[s, t] = (first block, second block, flag, direction): every contact of the tile has its first disk in block tile_info[s, t, 0] of slab s and its second in block tile_info[s, t, 1] of slab s + tile_info[s, t, 2], cyclically over 4 slabs. The flag is 0 or 1, the direction 0 to 5, the two blocks differ, and in each slab every block is the first block of exactly 2 tiles.
All inputs are finite; a program needn't handle non-finite values.
Results may differ from a plain program's by a relative error of at most 0.00012.
Values sent between devices are 32-bit elements; how exact they have to be, the bound alone decides.
A program may use at most 64 MiB of HBM per device.

v0:
```python
import math

import jax
import jax.numpy as jnp
from jax import lax
from jax.sharding import PartitionSpec as P

ITERS = 2


ANGLE_STEP = math.pi / 6.0
EPS = 1e-06


def shifted(block, axis, distance):
    devices = range(lax.axis_size(axis))
    route = [((i - distance) % len(devices), i) for i in devices]
    return lax.ppermute(block, axis, route)


def lane_tables(lane_ids):
    lane_index = jnp.arange(lane_ids.shape[-1], dtype=jnp.int32)
    return (lane_index[None, None, :, None] == lane_ids[:, :, None, :]).astype(jnp.float32)


def tile_normals(listing):
    angles = listing[:, 3].astype(jnp.float32) * ANGLE_STEP
    return jnp.stack([jnp.cos(angles), jnp.sin(angles)], axis=1)


def select(block_rows, lane_table):
    return jnp.einsum("xclk,xkm->xclm", block_rows, lane_table, precision=lax.Precision.HIGHEST)


def spread(values, lane_table):
    return jnp.einsum("xclm,xkm->xclk", values, lane_table, precision=lax.Precision.HIGHEST)


def contributions(weighted, normal, tables):
    values = normal[:, :, None, None] * weighted[:, None]
    return (spread(values, tables[:, 0]), spread(values, tables[:, 1]))


def deposit(first_part, second_part, first_ids, second_ids, side_ids, row_begin, row_count):
    pos_first = jnp.where(
        (first_ids >= row_begin) & (first_ids < row_begin + row_count), first_ids, row_count
    )
    pos_second = jnp.where(
        (second_ids >= row_begin) & (second_ids < row_begin + row_count), second_ids, row_count
    )
    buffer = jnp.zeros((row_count, 2) + first_part.shape[1:], jnp.float32)
    buffer = buffer.at[pos_first, 0].add(first_part, mode="drop")
    return buffer.at[pos_second, side_ids].add(-second_part, mode="drop")


def force_squares(values):
    return jnp.sum(values * values, axis=(0, 1, 3))


def image_squares(values):
    return jnp.sum(values * values, axis=(0, 1, 2, 4))


def local(loads, stiffness, tile_info, offsets):
    listing = tile_info[0]
    first_block = listing[:, 0]
    second_block = listing[:, 1]
    upper_flag = listing[:, 2]
    normal = tile_normals(listing)
    tables = lane_tables(offsets[0])
    spring = stiffness[0]
    block_count = loads.shape[1]

    def transpose_apply(disk_field):
        above_rows = shifted(disk_field, "row", -1)
        own_slab, upper_slab = (
            lax.all_gather(disk_field, "col", axis=1, tiled=True),
            lax.all_gather(above_rows, "col", axis=1, tiled=True),
        )
        own_slab = own_slab[0]
        upper_slab = upper_slab[0]
        first_rows = own_slab[first_block]
        second_rows = jnp.where(
            upper_flag[:, None, None, None] == 1, upper_slab[second_block], own_slab[second_block]
        )
        difference = select(first_rows, tables[:, 0]) - select(second_rows, tables[:, 1])
        projected = (
            normal[:, 0, None, None] * difference[:, 0]
            + normal[:, 1, None, None] * difference[:, 1]
        )
        return (spring[:, None, :] * projected)[None]

    def force_total(values):
        return lax.psum(force_squares(values), ("col", "row"))

    residual = loads
    search = transpose_apply(residual)
    forces = jnp.zeros_like(search)
    direction = search
    force_sq = force_total(search)
    for iteration in range(ITERS):
        weighted = spring[:, None, :] * direction[0]
        first_part, second_part = contributions(weighted, normal, tables)
        summed = lax.psum_scatter(
            deposit(
                first_part,
                second_part,
                first_block,
                second_block,
                upper_flag,
                jnp.int32(0),
                block_count * lax.axis_size("col"),
            ),
            "col",
            scatter_dimension=0,
            tiled=True,
        )
        lifted = shifted(summed[:, 1], "row", 1)
        image_field = (summed[:, 0] + lifted)[None]
        image_sq = lax.psum(image_squares(image_field), ("col", "row"))
        step_size = force_sq / (image_sq + EPS)
        forces = forces + step_size[:, None] * direction
        residual = residual - step_size[:, None] * image_field
        if iteration + 1 < ITERS:
            search = transpose_apply(residual)
            force_next = force_total(search)
            direction = search + (force_next / (force_sq + EPS))[:, None] * direction
            force_sq = force_next
    return (forces, residual)


def solution(mesh):
    placed = (
        P("row", "col", None, None, None),
        P("row", "col", None),
        P("row", "col", None),
        P("row", "col", None, None),
    )
    return jax.shard_map(
        local,
        mesh=mesh,
        in_specs=placed,
        out_specs=(P("row", "col", None, None), P("row", "col", None, None, None)),
        check_vma=False,
    )
```

profile of v0, /device:TPU:0, one launch (start us, length us, event | category | flops | bytes accessed | tf_op | source)
XLA Modules:
  0.0 419.9 jit_solution(14719931095018939203)
XLA Ops:
  7.2 2.5 collective-permute-start
  10.3 31.5 %all_gather.12 = f32[1,16,2,16,128]{4,3,2,0,1:T(8,128)S(1)} all-gather(f32[1,2,2,16,128]{4,3,2,0,1:T(8,128)} %bitcast.155), channel_id=1, replica_groups=mesh['col'=8,'row'=4] {'col'}, dimensions={1}, use_global_device_ids=true | all-gather | bytes 294912 | tf_op jit(solution)/shard_map/all_gather | solution.py:77
  44.0 30.7 %all_gather.13 = f32[1,16,2,16,128]{4,3,2,0,1:T(8,128)S(1)} all-gather(f32[1,2,2,16,128]{4,3,2,0,1:T(8,128)S(1)} %collective-permute-done), channel_id=1, replica_groups=mesh['col'=8,'row'=4] {'col'}, dimensions={1}, use_global_device_ids=true | all-gather | bytes 294912 | tf_op jit(solution)/shard_map/all_gather | solution.py:78
  75.6 0.7 copy-done.3
  77.2 0.7 scatter_fusion
  77.9 0.7 scatter_fusion.1
  78.6 0.8 copy-done
  79.4 63.5 %reduce-scatter.5.cloned.1.call-done = f32[2,2,2,16,128]{4,3,2,1,0:T(8,128)} async-done(((f32[16,2,2,16,128]{4,3,2,1,0:T(8,128)}), f32[2,2,2,16,128]{4,3,2,1,0:T(8,128)}) %reduce-scatter.5.cloned.1.call-update) | async-done | bytes 65552 | tf_op jit(solution)/shard_map/reduce_scatter | solution.py:104
  142.9 0.8 slice_bitcast_fusion
  144.0 3.1 collective-permute-done.1
  147.2 40.0 %all-reduce.2 = (f32[16]{0:T(128)S(1)}, f32[16]{0:T(128)S(1)}) all-reduce(f32[16]{0:T(128)S(1)} %multiply_reduce_fusion.3, f32[16]{0:T(128)S(1)} %multiply_reduce_fusion.2), channel_id=1, replica_groups=mesh['col'=8,'row'=4] {'col','row'}, use_global_device_ids=true, to_apply=%region_1.2 | all-reduce | flops 32 | bytes 256 | tf_op jit(solution)/shard_map/psum | solution.py:94
  187.4 30.9 %all_gather.14 = f32[1,16,2,16,128]{4,3,2,0,1:T(8,128)S(1)} all-gather(f32[1,2,2,16,128]{4,3,2,0,1:T(8,128)S(1)} %bitcast.153), channel_id=1, replica_groups=mesh['col'=8,'row'=4] {'col'}, dimensions={1}, use_global_device_ids=true | all-gather | bytes 294912 | tf_op jit(solution)/shard_map/all_gather | solution.py:77
  219.6 30.8 %all_gather.15 = f32[1,16,2,16,128]{4,3,2,0,1:T(8,128)S(1)} all-gather(f32[1,2,2,16,128]{4,3,2,0,1:T(8,128)S(1)} %bitcast.164), channel_id=1, replica_groups=mesh['col'=8,'row'=4] {'col'}, dimensions={1}, use_global_device_ids=true | all-gather | bytes 294912 | tf_op jit(solution)/shard_map/all_gather | solution.py:78
  251.5 37.7 %psum.30 = f32[16]{0:T(128)S(1)} all-reduce(f32[16]{0:T(128)S(1)} %multiply_reduce_fusion.1), channel_id=1, replica_groups=mesh['col'=8,'row'=4] {'col','row'}, use_global_device_ids=true, to_apply=%region_8.9 | all-reduce | flops 16 | bytes 128 | tf_op jit(solution)/shard_map/psum | solution.py:94
  290.1 0.7 scatter_fusion.2
  290.8 0.7 scatter_fusion.3
  291.5 0.9 copy.34
  294.3 72.2 %all-reduce.5.cloned.1.call-done = f32[16,2,2,16,128]{4,3,2,0,1:T(8,128)} async-done(((f32[16,2,2,16,128]{4,3,2,0,1:T(8,128)}), f32[16,2,2,16,128]{4,3,2,0,1:T(8,128)}) %all-reduce.5.cloned.1.call-update) | async-done | bytes 524304
  366.5 0.8 dynamic-slice_bitcast_fusion
  367.2 3.3 collective-permute-done.3
  370.6 0.9 multiply_reduce_fusion
  371.4 39.4 %psum.31 = f32[16]{0:T(128)S(1)} all-reduce(f32[16]{0:T(128)S(1)} %multiply_reduce_fusion), channel_id=1, replica_groups=mesh['col'=8,'row'=4] {'col','row'}, use_global_device_ids=true, to_apply=%region_13.14 | all-reduce | flops 16 | bytes 128 | tf_op jit(solution)/shard_map/psum | solution.py:120
  410.9 0.7 multiply_add_fusion
  411.6 1.4 bitcast_subtract_fusion
  (55 shorter events, 9.5 us)
Async XLA Ops:
  7.2 2.5 copy-start.4
  7.2 135.8 %reduce-scatter.5.cloned.1.call-start = ((), (), s32[]{:S(2)}) async-start(), calls=%async_computation.1 | async-start | bytes 589824 | tf_op jit(solution)/shard_map/reduce_scatter | solution.py:104
  7.2 36.8 %collective-permute-start = (f32[1,2,2,16,128]{4,3,2,0,1:T(8,128)}, f32[1,2,2,16,128]{4,3,2,0,1:T(8,128)S(1)}, u32[]{:S(2)}, u32[]{:S(2)}) collective-permute-start(f32[1,2,2,16,128]{4,3,2,0,1:T(8,128)} %bitcast.154), channel_id=1, source_target_pairs={{1,0},{2,1},{3,2},{0,3},{5,4},{6,5},{7,6},{4,7},{9,8},{10,9},{11,1... | collective-permute-start | bytes 98312 | tf_op jit(solution)/shard_map/ppermute | solution.py:18
  41.8 0.7 copy-start.5
  75.6 0.7 copy-start.3
  78.6 0.8 copy-start
  79.4 287.1 %all-reduce.5.cloned.1.call-start = ((), (), s32[]{:S(2)}) async-start(), calls=%async_computation.2 | async-start | bytes 1048576
  142.9 4.2 copy-start.1
  143.8 3.3 collective-permute-start.1
  144.0 43.3 %copy-start.2 = (f32[1,2,2,16,128]{4,3,2,1,0:T(8,128)S(1)}, f32[1,2,2,16,128]{4,3,2,1,0:T(8,128)}, u32[]{:S(2)}) copy-start(f32[1,2,2,16,128]{4,3,2,1,0:T(8,128)} %param.4) | copy-start | bytes 98308
  187.4 32.3 %collective-permute-start.2 = (f32[1,2,2,16,128]{4,3,2,1,0:T(8,128)S(1)}, f32[1,2,2,16,128]{4,3,2,1,0:T(8,128)S(1)}, u32[]{:S(2)}, u32[]{:S(2)}) collective-permute-start(f32[1,2,2,16,128]{4,3,2,1,0:T(8,128)S(1)} %bitcast_subtract_fusion.1), channel_id=1, source_target_pairs={{1,0},{2,1},{3,2},{0,3},{5,4},{6,5},{7,6},{4,7},{9,8},{10,9},{11,1... | collective-permute-start | bytes 98312 | tf_op jit(solution)/shard_map/ppermute | solution.py:18
  292.4 0.7 copy-start.6
  367.2 3.3 collective-permute-start.3
Sparse Core Ops, SparseCore 0:
  79.5 63.3 reduce-scatter.4
  292.5 73.9 all-reduce.4
where the time goes:
time: 421 us; the launch traced here: 420 us
  blocking collectives  241 us (57%)
  waiting for transfers between devices  142 us (34%)
  between operations  14.9 us (4%)
  local copies, waits for them, and re-layouts  9.26 us (2%)
  other arithmetic  7.34 us (2%)
    psum x2, blocking collectives, force_total(): return lax.psum(force_squares(values), ('col', 'row'))  77.8 us
    unnamed x3, waiting for transfers between devices  72.2 us
    reduce_scatter x1, waiting for transfers between devices, local(): lax.psum_scatter(deposit(first_part, second_part, first_block, second_blo...  63.5 us
    all_gather x2, blocking collectives, transpose_apply(): lax.all_gather(disk_field, 'col', axis=1, tiled=True)  62.4 us
    all_gather x2, blocking collectives, transpose_apply(): lax.all_gather(above_rows, 'col', axis=1, tiled=True)  61.5 us
    psum x1, blocking collectives, local(): image_sq = lax.psum(image_squares(image_field), ('col', 'row'))  39.4 us
  transfers between devices with their start and end apart: 6, of which 4 were waited for; matrix products, arithmetic and copies ran while one was open for 1% of the time, Pallas kernels for 0%

commit v1 on v0

--- a/solution.py
+++ b/solution.py
@@ -1,8 +1,12 @@
+import functools
 import math
 
 import jax
 import jax.numpy as jnp
+import numpy as np
 from jax import lax
+from jax.experimental import pallas as pl
+from jax.experimental.pallas import tpu as pltpu
 from jax.sharding import PartitionSpec as P
 
 ITERS = 2
@@ -129,6 +133,288 @@
     return (forces, residual)
 
 
+MESH = pl.DeviceIdType.MESH
+CORES = 2
+SIDE = 2
+UNROLL_CHUNKS = 2
+REPLICATED_LIMIT = 8 * 1024 * 1024
+COSINES = [float(v) for v in np.cos(np.arange(6, dtype=np.float32) * np.float32(ANGLE_STEP))]
+SINES = [float(v) for v in np.sin(np.arange(6, dtype=np.float32) * np.float32(ANGLE_STEP))]
+
+
+def gather_kernel(line, cols, x_ref, out_ref, send_sem, recv_sem, local_sem):
+    col, row = lax.axis_index("col"), lax.axis_index("row")
+    z, x = col // SIDE, lax.rem(col, SIDE)
+    y, c = row // CORES, lax.rem(row, CORES)
+    xa, ya = x + (1 - c) * (1 - 2 * x), y + c * (1 - 2 * y)
+    xb, yb = x + c * (1 - 2 * x), y + (1 - c) * (1 - 2 * y)
+
+    def device(zz, xx, yy, cc):
+        return {"col": zz * SIDE + xx, "row": yy * CORES + cc}
+
+    def chunk(zz, xx, yy, cc):
+        return (yy * CORES + cc) * cols + zz * SIDE + xx
+
+    along = [lax.rem(z + step, line) for step in range(line)]
+    partner_a, partner_b = device(z, xa, ya, c), device(z, xb, yb, c)
+    partner_core = device(z, x, y, 1 - c)
+
+    barrier = pltpu.get_barrier_semaphore()
+    peers = [device(zz, x, y, c) for zz in along[1:]] + [partner_a, partner_b, partner_core]
+    for peer in peers:
+        pl.semaphore_signal(barrier, inc=1, device_id=peer, device_id_type=MESH)
+    me = chunk(z, x, y, c)
+    keep = pltpu.make_async_copy(x_ref, out_ref.at[me], local_sem)
+    keep.start()
+    pl.semaphore_wait(barrier, len(peers))
+
+    sent = []
+
+    def send(index, peer, own=False):
+        copy = pltpu.make_async_remote_copy(
+            src_ref=x_ref if own else out_ref.at[index],
+            dst_ref=out_ref.at[index],
+            send_sem=send_sem.at[len(sent)],
+            recv_sem=recv_sem.at[index],
+            device_id=peer,
+            device_id_type=MESH,
+        )
+        copy.start()
+        sent.append(copy)
+
+    def arrive(index):
+        pltpu.make_async_remote_copy(
+            src_ref=x_ref,
+            dst_ref=out_ref.at[index],
+            send_sem=send_sem.at[0],
+            recv_sem=recv_sem.at[index],
+            device_id=partner_core,
+            device_id_type=MESH,
+        ).wait_recv()
+
+    for zz in along[1:]:
+        send(me, device(zz, x, y, c), own=True)
+    for peer in (partner_a, partner_b, partner_core):
+        send(me, peer, own=True)
+    order = [along[0]] + [along[s] for s in (1, line - 1)] + [along[s] for s in range(2, line - 1)]
+    for position, zz in enumerate(order):
+        if position:
+            index = chunk(zz, x, y, c)
+            arrive(index)
+            for peer in (partner_a, partner_b, partner_core):
+                send(index, peer)
+    for zz in order:
+        index = chunk(zz, xa, ya, c)
+        arrive(index)
+        send(index, partner_b)
+        send(index, partner_core)
+    for zz in order:
+        index = chunk(zz, xb, yb, c)
+        arrive(index)
+        send(index, partner_core)
+    for zz in order:
+        index = chunk(zz, 1 - x, 1 - y, c)
+        arrive(index)
+        send(index, partner_core)
+    for xx, yy in ((x, y), (xa, ya), (xb, yb), (1 - x, 1 - y)):
+        for zz in order:
+            arrive(chunk(zz, xx, yy, 1 - c))
+    for copy in sent:
+        copy.wait_send()
+    keep.wait()
+
+
+def solve_kernel(
+    dims, info_ref, place_ref, all_ref, forces_ref, left_ref,
+    search_a, search_b, image_a, image_b, rest_ref, cos_ref, sin_ref,
+):
+    slabs, blocks, per_blocks, per_tiles, cases, lanes = dims
+    chunks = all_ref.shape[0]
+    disk_rows = 2 * cases
+    cols = chunks // slabs
+    base = per_blocks * disk_rows
+    for k in range(6):
+        cos_ref[k] = COSINES[k]
+        sin_ref[k] = SINES[k]
+
+    def apply_both(read_block, search_ref, image_ref):
+        image_ref[...] = jnp.zeros_like(image_ref)
+        sub = lax.broadcasted_iota(jnp.int32, (lanes, lanes), 0)
+
+        def body(step, total):
+            parts = []
+            for u in range(UNROLL_CHUNKS):
+                piece = step * UNROLL_CHUNKS + u
+                slab = piece // cols
+                for k in range(per_tiles):
+                    tile = piece * per_tiles + k
+                    first = slab * blocks + info_ref[tile * 4]
+                    upper = lax.rem(slab + info_ref[tile * 4 + 2], slabs)
+                    second = upper * blocks + info_ref[tile * 4 + 1]
+                    turn = info_ref[tile * 4 + 3]
+                    n0, n1 = cos_ref[turn], sin_ref[turn]
+                    spring = all_ref[piece, base + k : base + k + 1, :]
+                    at = base + per_tiles + 2 * k
+                    lane_i = all_ref[piece, at : at + 1, :].astype(jnp.int32)
+                    lane_j = all_ref[piece, at + 1 : at + 2, :].astype(jnp.int32)
+                    vi, vj = read_block(first), read_block(second)
+                    pi = n0 * vi[:cases] + n1 * vi[cases:]
+                    pj = n0 * vj[:cases] + n1 * vj[cases:]
+                    gi = jnp.take_along_axis(
+                        pi, jnp.broadcast_to(lane_i, pi.shape), axis=1, mode="promise_in_bounds"
+                    )
+                    gj = jnp.take_along_axis(
+                        pj, jnp.broadcast_to(lane_j, pj.shape), axis=1, mode="promise_in_bounds"
+                    )
+                    value = spring * (gi - gj)
+                    search_ref[tile] = value
+                    total = total + value * value
+                    weighted = spring * value
+                    high = weighted.astype(jnp.bfloat16)
+                    rest = weighted - high.astype(jnp.float32)
+                    middle = rest.astype(jnp.bfloat16)
+                    low = (rest - middle.astype(jnp.float32)).astype(jnp.bfloat16)
+                    lhs = jnp.concatenate([high, middle, low], axis=0)
+                    hot = jnp.concatenate(
+                        [
+                            jnp.where(sub == lane_i, 1.0, 0.0).astype(jnp.bfloat16),
+                            jnp.where(sub == lane_j, 1.0, 0.0).astype(jnp.bfloat16),
+                        ],
+                        axis=0,
+                    )
+                    out = lax.dot_general(
+                        lhs, hot, (((1,), (1,)), ((), ())), preferred_element_type=jnp.float32
+                    )
+                    out = out[:cases] + (out[cases : 2 * cases] + out[2 * cases :])
+                    parts.append((first, second, n0, n1, out[:, :lanes], out[:, lanes:]))
+            for first, second, n0, n1, one, two in parts:
+                image_ref[first, :cases] += n0 * one
+                image_ref[first, cases:] += n1 * one
+                image_ref[second, :cases] -= n0 * two
+                image_ref[second, cases:] -= n1 * two
+            return total
+
+        total = lax.fori_loop(
+            0, chunks // UNROLL_CHUNKS, body, jnp.zeros((cases, lanes), jnp.float32)
+        )
+        return jnp.sum(total, axis=1, keepdims=True)
+
+    def chunk_rows(block):
+        start = pl.multiple_of(lax.rem(block, per_blocks) * disk_rows, 8)
+        return all_ref[block // per_blocks, pl.ds(start, disk_rows), :]
+
+    def squares(field):
+        both = jnp.sum(field * field, axis=0)
+        return both[:cases] + both[cases:]
+
+    def over_chunks(visit):
+        return jnp.sum(
+            lax.fori_loop(
+                0, chunks, visit, jnp.zeros((cases, lanes), jnp.float32), unroll=2
+            ),
+            axis=1,
+            keepdims=True,
+        )
+
+    gamma = apply_both(chunk_rows, search_a, image_a)
+
+    def norm_first(piece, total):
+        return total + squares(image_a[pl.ds(piece * per_blocks, per_blocks)])
+
+    alpha = gamma / (over_chunks(norm_first) + EPS)
+    alpha_rows = jnp.concatenate([alpha, alpha], axis=0)
+
+    def renew(piece, carry):
+        for b in range(per_blocks):
+            block = piece * per_blocks + b
+            rest_ref[block] = (
+                all_ref[piece, b * disk_rows : (b + 1) * disk_rows, :]
+                - alpha_rows * image_a[block]
+            )
+        return carry
+
+    lax.fori_loop(0, chunks, renew, 0, unroll=2)
+    gamma_next = apply_both(lambda block: rest_ref[block], search_b, image_b)
+    beta = gamma_next / (gamma + EPS)
+    beta_rows = jnp.concatenate([beta, beta], axis=0)
+
+    def norm_second(piece, total):
+        span = pl.ds(piece * per_blocks, per_blocks)
+        return total + squares(image_b[span] + beta_rows * image_a[span])
+
+    alpha_next = gamma_next / (over_chunks(norm_second) + EPS)
+    alpha_next_rows = jnp.concatenate([alpha_next, alpha_next], axis=0)
+    place = place_ref[0]
+    for k in range(per_tiles):
+        tile = place * per_tiles + k
+        old = search_a[tile]
+        forces_ref[0, k] = alpha * old + alpha_next * (search_b[tile] + beta * old)
+    for b in range(per_blocks):
+        block = place * per_blocks + b
+        left = rest_ref[block] - alpha_next_rows * (image_b[block] + beta_rows * image_a[block])
+        left_ref[0, b, 0] = left[:cases]
+        left_ref[0, b, 1] = left[cases:]
+
+
+def replicated(cols, rows, loads, stiffness, tile_info, offsets):
+    per_blocks, cases, lanes = loads.shape[1], loads.shape[3], loads.shape[4]
+    per_tiles = stiffness.shape[1]
+    chunks = cols * rows
+    parts = [
+        loads.reshape(-1, lanes),
+        stiffness[0],
+        offsets.reshape(-1, lanes).astype(jnp.float32),
+        jnp.pad(tile_info[0].astype(jnp.float32), ((0, 0), (0, lanes - tile_info.shape[2]))),
+    ]
+    packed = jnp.concatenate(parts, axis=0)
+    height = packed.shape[0]
+    vmem = pl.BlockSpec(memory_space=pltpu.VMEM)
+    smem = pl.BlockSpec(memory_space=pltpu.SMEM)
+    everything = pl.pallas_call(
+        functools.partial(gather_kernel, cols // SIDE, cols),
+        out_shape=jax.ShapeDtypeStruct((chunks, height, lanes), jnp.float32),
+        in_specs=[vmem],
+        out_specs=vmem,
+        scratch_shapes=[
+            pltpu.SemaphoreType.DMA((chunks,)),
+            pltpu.SemaphoreType.DMA((chunks,)),
+            pltpu.SemaphoreType.DMA,
+        ],
+        compiler_params=pltpu.CompilerParams(collective_id=0, has_side_effects=True),
+    )(packed)
+    info = everything[:, height - per_tiles :, :4].astype(jnp.int32).reshape(-1)
+    place = (lax.axis_index("row") * cols + lax.axis_index("col")).astype(jnp.int32)
+    disk = (chunks * per_blocks, 2 * cases, lanes)
+    contact = (chunks * per_tiles, cases, lanes)
+    dims = (rows, cols * per_blocks, per_blocks, per_tiles, cases, lanes)
+    return pl.pallas_call(
+        functools.partial(solve_kernel, dims),
+        out_shape=(
+            jax.ShapeDtypeStruct((1, per_tiles, cases, lanes), jnp.float32),
+            jax.ShapeDtypeStruct(loads.shape, jnp.float32),
+        ),
+        in_specs=[smem, smem, vmem],
+        out_specs=(vmem, vmem),
+        scratch_shapes=[
+            pltpu.VMEM(contact, jnp.float32),
+            pltpu.VMEM(contact, jnp.float32),
+            pltpu.VMEM(disk, jnp.float32),
+            pltpu.VMEM(disk, jnp.float32),
+            pltpu.VMEM(disk, jnp.float32),
+            pltpu.SMEM((6,), jnp.float32),
+            pltpu.SMEM((6,), jnp.float32),
+        ],
+        compiler_params=pltpu.CompilerParams(vmem_limit_bytes=32 * 1024 * 1024),
+    )(info, place[None], everything)
+
+
+def program_body(cols, rows, loads, stiffness, tile_info, offsets):
+    whole = cols * rows * loads.size * 4
+    if whole <= REPLICATED_LIMIT and cols % SIDE == 0 and rows == SIDE * CORES:
+        return replicated(cols, rows, loads, stiffness, tile_info, offsets)
+    return local(loads, stiffness, tile_info, offsets)
+
+
 def solution(mesh):
     placed = (
         P("row", "col", None, None, None),
@@ -137,7 +423,7 @@
         P("row", "col", None, None),
     )
     return jax.shard_map(
-        local,
+        functools.partial(program_body, mesh.shape["col"], mesh.shape["row"]),
         mesh=mesh,
         in_specs=placed,
         out_specs=(P("row", "col", None, None), P("row", "col", None, None, None)),

time: 421 us -> 42.5 us (0.10)
  blocking collectives: 241 us -> 0 us
  waiting for transfers between devices: 142 us -> 0 us
  Pallas kernels: 0 us -> 36.3 us
  between operations: 14.9 us -> 0.66 us
  local copies, waits for them, and re-layouts: 9.26 us -> 1.43 us
    all_gather x4 -> x0, blocking collectives: 124 us -> none  [the longest x2 62.4 us: transpose_apply(): lax.all_gather(disk_field, 'col', axis=1, tiled=True)]
    psum x3 -> x0, blocking collectives: 117 us -> none  [the longest x2 77.8 us: force_total(): return lax.psum(force_squares(values), ('col', 'row'))]
    unnamed x3 -> x0, waiting for transfers between devices: 72.2 us -> none
    reduce_scatter x1 -> x0, waiting for transfers between devices: 63.5 us -> none  [local(): lax.psum_scatter(deposit(first_part, second_part, first_block, second_blo...]
    pallas_call x0 -> x2, Pallas kernels: none -> 36.3 us  [the longest x1 20.9 us: replicated(): pl.pallas_call(functools.partial(gather_kernel, cols // SIDE, cols), out_...]
    ppermute x4 -> x0, waiting for transfers between devices: 6.48 us -> none  [shifted(): return lax.ppermute(block, axis, route)]
  transfers between devices with their start and end apart: 6 -> 0, of which waited for: 4 -> 0; matrix products, arithmetic and copies ran while one was open for 1% -> 0% of each run, Pallas kernels for 0% -> 0%
where the time goes in v1:
time: 42.5 us; the launch traced here: 42.1 us
  Pallas kernels  36.3 us (85%)
  other arithmetic  3.69 us (9%)
  local copies, waits for them, and re-layouts  1.43 us (3%)
  between operations  0.66 us (2%)
    pallas_call x1, Pallas kernels, replicated(): pl.pallas_call(functools.partial(gather_kernel, cols // SIDE, cols), out_...  20.9 us
    pallas_call x1, Pallas kernels, replicated(): pl.pallas_call(functools.partial(solve_kernel, dims), out_shape=(jax.Shap...  15.4 us
    concatenate x1, other arithmetic, replicated(): packed = jnp.concatenate(parts, axis=0)  1.39 us
    unnamed x2, local copies, waits for them, and re-layouts  1.31 us
    convert_element_type x1, other arithmetic, replicated(): info = everything[:, height - per_tiles:, :4].astype(jnp.int32).reshape(-1)  0.93 us

profile of v1, /device:TPU:0, one launch (start us, length us, event | category | flops | bytes accessed | tf_op | source)
XLA Modules:
  0.0 42.1 jit_solution(3164523777115272076)
XLA Ops:
  0.6 0.7 %convert_bitcast_fusion = f32[4,4]{1,0:T(4,128)S(1)} fusion(s32[1,4,4]{2,1,0:T(4,128)} %param.6), kind=kLoop, calls=%fused_computation.3 | loop fusion | flops 16 | bytes 128 | tf_op jit(solution)/shard_map/convert_element_type | solution.py:367
  1.3 0.7 %convert_element_type.17 = f32[1,4,2,128]{3,2,1,0:T(2,128)S(1)} convert(s32[1,4,2,128]{3,2,1,0:T(2,128)} %param.7) | non-fusion elementwise | flops 1024 | bytes 8192 | tf_op jit(solution)/shard_map/convert_element_type | solution.py:366
  2.0 1.4 %select_maximum_fusion.x_ref = f32[80,128]{1,0:T(8,128)} fusion(f32[4,4]{1,0:T(4,128)S(1)} %convert_bitcast_fusion, f32[8,128]{1,0:T(8,128)S(1)} %bitcast.7, f32[4,128]{1,0:T(4,128)} %bitcast.8, f32[64,128]{1,0:T(8,128)} %bitcast.6), kind=kLoop, calls=%fused_computation.1 | loop fusion | flops 51200 | bytes 79936 | tf_op jit(solution)/shard_map/concatenate | solution.py:369
  3.4 20.9 %shard_map.59.all_ref = f32[32,80,128]{2,1,0:T(8,128)} custom-call(f32[80,128]{1,0:T(8,128)} %select_maximum_fusion.x_ref), custom_call_target="tpu_custom_call" | custom-call | tf_op jit(solution)/shard_map/pallas_call | solution.py:373
  24.3 0.9 %slice_convert_fusion = s32[32,4,4]{2,1,0:T(4,128)S(1)} fusion(f32[32,80,128]{2,1,0:T(8,128)} %shard_map.59.all_ref), kind=kLoop, calls=%fused_computation | loop fusion | flops 512 | bytes 4096 | tf_op jit(solution)/shard_map/convert_element_type | solution.py:385
  25.2 0.1 reshape.14.info_ref
  25.3 0.0 copy-start
  25.4 1.3 %copy-done = f32[32,80,128]{2,1,0:T(8,128)S(1)} copy-done((f32[32,80,128]{2,1,0:T(8,128)S(1)}, f32[32,80,128]{2,1,0:T(8,128)}, u32[]{:S(2)}) %copy-start) | copy-done | bytes 1310744
  26.7 15.4 %shard_map.60 = (f32[1,4,16,128]{3,2,1,0:T(8,128)}, f32[1,2,2,16,128]{4,3,2,1,0:T(8,128)}) custom-call(s32[512]{0:T(512)S(1)} %reshape.14.info_ref, s32[1]{0:T(128)} %bitcast.4.place_ref, f32[32,80,128]{2,1,0:T(8,128)S(1)} %copy-done), custom_call_target="tpu_custom_call" | custom-call | tf_op jit(solution)/shard_map/pallas_call | solution.py:390
Async XLA Ops:
  25.3 1.3 %copy-start = (f32[32,80,128]{2,1,0:T(8,128)S(1)}, f32[32,80,128]{2,1,0:T(8,128)}, u32[]{:S(2)}) copy-start(f32[32,80,128]{2,1,0:T(8,128)} %shard_map.59.all_ref) | copy-start | bytes 3932164

commit v2 on v1

--- a/solution.py
+++ b/solution.py
@@ -136,13 +136,17 @@
 MESH = pl.DeviceIdType.MESH
 CORES = 2
 SIDE = 2
-UNROLL_CHUNKS = 2
+UNROLL_CHUNKS = 4
+INFO_ROW = 8
+SPRING_ROW = 12
 REPLICATED_LIMIT = 8 * 1024 * 1024
 COSINES = [float(v) for v in np.cos(np.arange(6, dtype=np.float32) * np.float32(ANGLE_STEP))]
 SINES = [float(v) for v in np.sin(np.arange(6, dtype=np.float32) * np.float32(ANGLE_STEP))]
 
 
-def gather_kernel(line, cols, x_ref, out_ref, send_sem, recv_sem, local_sem):
+def gather_kernel(
+    line, cols, loads_ref, spring_ref, info_ref, lanes_ref, out_ref, send_sem, recv_sem
+):
     col, row = lax.axis_index("col"), lax.axis_index("row")
     z, x = col // SIDE, lax.rem(col, SIDE)
     y, c = row // CORES, lax.rem(row, CORES)
@@ -164,15 +168,22 @@
     for peer in peers:
         pl.semaphore_signal(barrier, inc=1, device_id=peer, device_id_type=MESH)
     me = chunk(z, x, y, c)
-    keep = pltpu.make_async_copy(x_ref, out_ref.at[me], local_sem)
-    keep.start()
+    disk_rows, lanes = loads_ref.shape
+    tiles, words = info_ref.shape
+    out_ref[me, :disk_rows] = loads_ref[...]
+    out_ref[me, disk_rows : disk_rows + 2 * tiles] = lanes_ref[...].astype(jnp.float32)
+    out_ref[me, disk_rows + INFO_ROW : disk_rows + SPRING_ROW] = jnp.zeros((tiles, lanes), jnp.float32)
+    numbers = info_ref[...].astype(jnp.float32)
+    listing = jnp.concatenate([numbers[k : k + 1] for k in range(tiles)], axis=1)
+    out_ref[me, disk_rows + INFO_ROW : disk_rows + INFO_ROW + 1, : tiles * words] = listing
+    out_ref[me, disk_rows + SPRING_ROW : disk_rows + SPRING_ROW + tiles] = spring_ref[...]
     pl.semaphore_wait(barrier, len(peers))
 
     sent = []
 
-    def send(index, peer, own=False):
+    def send(index, peer):
         copy = pltpu.make_async_remote_copy(
-            src_ref=x_ref if own else out_ref.at[index],
+            src_ref=out_ref.at[index],
             dst_ref=out_ref.at[index],
             send_sem=send_sem.at[len(sent)],
             recv_sem=recv_sem.at[index],
@@ -184,7 +195,7 @@
 
     def arrive(index):
         pltpu.make_async_remote_copy(
-            src_ref=x_ref,
+            src_ref=out_ref.at[index],
             dst_ref=out_ref.at[index],
             send_sem=send_sem.at[0],
             recv_sem=recv_sem.at[index],
@@ -193,9 +204,9 @@
         ).wait_recv()
 
     for zz in along[1:]:
-        send(me, device(zz, x, y, c), own=True)
+        send(me, device(zz, x, y, c))
     for peer in (partner_a, partner_b, partner_core):
-        send(me, peer, own=True)
+        send(me, peer)
     order = [along[0]] + [along[s] for s in (1, line - 1)] + [along[s] for s in range(2, line - 1)]
     for position, zz in enumerate(order):
         if position:
@@ -221,21 +232,25 @@
             arrive(chunk(zz, xx, yy, 1 - c))
     for copy in sent:
         copy.wait_send()
-    keep.wait()
 
 
 def solve_kernel(
-    dims, info_ref, place_ref, all_ref, forces_ref, left_ref,
-    search_a, search_b, image_a, image_b, rest_ref, cos_ref, sin_ref,
+    dims, place_ref, all_ref, forces_ref, left_ref,
+    search_a, search_b, image_a, image_b, rest_ref, info_ref, cos_ref, sin_ref, info_sem,
 ):
     slabs, blocks, per_blocks, per_tiles, cases, lanes = dims
     chunks = all_ref.shape[0]
     disk_rows = 2 * cases
     cols = chunks // slabs
     base = per_blocks * disk_rows
+    listing = pltpu.make_async_copy(
+        all_ref.at[:, base + INFO_ROW : base + INFO_ROW + 1, :], info_ref, info_sem
+    )
+    listing.start()
     for k in range(6):
         cos_ref[k] = COSINES[k]
         sin_ref[k] = SINES[k]
+    listing.wait()
 
     def apply_both(read_block, search_ref, image_ref):
         image_ref[...] = jnp.zeros_like(image_ref)
@@ -248,13 +263,14 @@
                 slab = piece // cols
                 for k in range(per_tiles):
                     tile = piece * per_tiles + k
-                    first = slab * blocks + info_ref[tile * 4]
-                    upper = lax.rem(slab + info_ref[tile * 4 + 2], slabs)
-                    second = upper * blocks + info_ref[tile * 4 + 1]
-                    turn = info_ref[tile * 4 + 3]
+                    info = [info_ref[piece, 0, 4 * k + w].astype(jnp.int32) for w in range(4)]
+                    first = slab * blocks + info[0]
+                    upper = lax.rem(slab + info[2], slabs)
+                    second = upper * blocks + info[1]
+                    turn = info[3]
                     n0, n1 = cos_ref[turn], sin_ref[turn]
-                    spring = all_ref[piece, base + k : base + k + 1, :]
-                    at = base + per_tiles + 2 * k
+                    spring = all_ref[piece, base + SPRING_ROW + k : base + SPRING_ROW + k + 1, :]
+                    at = base + 2 * k
                     lane_i = all_ref[piece, at : at + 1, :].astype(jnp.int32)
                     lane_j = all_ref[piece, at + 1 : at + 2, :].astype(jnp.int32)
                     vi, vj = read_block(first), read_block(second)
@@ -360,29 +376,20 @@
     per_blocks, cases, lanes = loads.shape[1], loads.shape[3], loads.shape[4]
     per_tiles = stiffness.shape[1]
     chunks = cols * rows
-    parts = [
-        loads.reshape(-1, lanes),
-        stiffness[0],
-        offsets.reshape(-1, lanes).astype(jnp.float32),
-        jnp.pad(tile_info[0].astype(jnp.float32), ((0, 0), (0, lanes - tile_info.shape[2]))),
-    ]
-    packed = jnp.concatenate(parts, axis=0)
-    height = packed.shape[0]
+    height = 2 * per_blocks * cases + SPRING_ROW + per_tiles
     vmem = pl.BlockSpec(memory_space=pltpu.VMEM)
     smem = pl.BlockSpec(memory_space=pltpu.SMEM)
     everything = pl.pallas_call(
         functools.partial(gather_kernel, cols // SIDE, cols),
         out_shape=jax.ShapeDtypeStruct((chunks, height, lanes), jnp.float32),
-        in_specs=[vmem],
+        in_specs=[vmem] * 4,
         out_specs=vmem,
         scratch_shapes=[
             pltpu.SemaphoreType.DMA((chunks,)),
             pltpu.SemaphoreType.DMA((chunks,)),
-            pltpu.SemaphoreType.DMA,
         ],
         compiler_params=pltpu.CompilerParams(collective_id=0, has_side_effects=True),
-    )(packed)
-    info = everything[:, height - per_tiles :, :4].astype(jnp.int32).reshape(-1)
+    )(loads.reshape(-1, lanes), stiffness[0], tile_info[0], offsets.reshape(-1, lanes))
     place = (lax.axis_index("row") * cols + lax.axis_index("col")).astype(jnp.int32)
     disk = (chunks * per_blocks, 2 * cases, lanes)
     contact = (chunks * per_tiles, cases, lanes)
@@ -393,7 +400,7 @@
             jax.ShapeDtypeStruct((1, per_tiles, cases, lanes), jnp.float32),
             jax.ShapeDtypeStruct(loads.shape, jnp.float32),
         ),
-        in_specs=[smem, smem, vmem],
+        in_specs=[smem, vmem],
         out_specs=(vmem, vmem),
         scratch_shapes=[
             pltpu.VMEM(contact, jnp.float32),
@@ -401,16 +408,18 @@
             pltpu.VMEM(disk, jnp.float32),
             pltpu.VMEM(disk, jnp.float32),
             pltpu.VMEM(disk, jnp.float32),
+            pltpu.SMEM((chunks, 1, lanes), jnp.float32),
             pltpu.SMEM((6,), jnp.float32),
             pltpu.SMEM((6,), jnp.float32),
+            pltpu.SemaphoreType.DMA,
         ],
         compiler_params=pltpu.CompilerParams(vmem_limit_bytes=32 * 1024 * 1024),
-    )(info, place[None], everything)
+    )(place[None], everything)
 
 
 def program_body(cols, rows, loads, stiffness, tile_info, offsets):
     whole = cols * rows * loads.size * 4
-    if whole <= REPLICATED_LIMIT and cols % SIDE == 0 and rows == SIDE * CORES:
+    if whole <= REPLICATED_LIMIT and cols % SIDE == 0 and rows == SIDE * CORES and stiffness.shape[1] == 4:
         return replicated(cols, rows, loads, stiffness, tile_info, offsets)
     return local(loads, stiffness, tile_info, offsets)
 

time: 42.5 us -> 36.6 us (0.86)
  other arithmetic: 3.69 us -> 0 us
  Pallas kernels: 36.3 us -> 34.4 us
    convert_element_type x3 -> x0, other arithmetic: 2.3 us -> none  [the longest x1 0.93 us: replicated(): info = everything[:, height - per_tiles:, :4].astype(jnp.int32).reshape(-1)]
    pallas_call x1, Pallas kernels: 15.4 us -> 13.5 us  [replicated(): pl.pallas_call(functools.partial(solve_kernel, dims), out_shape=(jax.Shap...]
    concatenate x1 -> x0, other arithmetic: 1.39 us -> none  [replicated(): packed = jnp.concatenate(parts, axis=0)]
where the time goes in v2:
time: 36.6 us; the launch traced here: 36.3 us
  Pallas kernels  34.4 us (94%)
  local copies, waits for them, and re-layouts  1.31 us (4%)
  between operations  0.65 us (2%)
    pallas_call x1, Pallas kernels, replicated(): pl.pallas_call(functools.partial(gather_kernel, cols // SIDE, cols), out_...  20.9 us
    pallas_call x1, Pallas kernels, replicated(): pl.pallas_call(functools.partial(solve_kernel, dims), out_shape=(jax.Shap...  13.5 us
    unnamed x2, local copies, waits for them, and re-layouts  1.31 us

profile of v2, /device:TPU:0, one launch (start us, length us, event | category | flops | bytes accessed | tf_op | source)
XLA Modules:
  0.0 36.3 jit_solution(13048431819673005340)
XLA Ops:
  0.6 20.9 %shard_map.59.all_ref = f32[32,80,128]{2,1,0:T(8,128)} custom-call(f32[64,128]{1,0:T(8,128)} %bitcast.5, f32[4,128]{1,0:T(4,128)} %bitcast.7, s32[4,4]{1,0:T(4,128)} %bitcast.8, s32[8,128]{1,0:T(8,128)} %bitcast.6), custom_call_target="tpu_custom_call" | custom-call | tf_op jit(solution)/shard_map/pallas_call | solution.py:382
  21.5 0.0 copy-start
  21.6 1.3 %copy-done = f32[32,80,128]{2,1,0:T(8,128)S(1)} copy-done((f32[32,80,128]{2,1,0:T(8,128)S(1)}, f32[32,80,128]{2,1,0:T(8,128)}, u32[]{:S(2)}) %copy-start) | copy-done | bytes 1310744
  22.9 13.5 %shard_map.60 = (f32[1,4,16,128]{3,2,1,0:T(8,128)}, f32[1,2,2,16,128]{4,3,2,1,0:T(8,128)}) custom-call(s32[1]{0:T(128)} %bitcast.place_ref, f32[32,80,128]{2,1,0:T(8,128)S(1)} %copy-done), custom_call_target="tpu_custom_call" | custom-call | tf_op jit(solution)/shard_map/pallas_call | solution.py:397
Async XLA Ops:
  21.5 1.3 %copy-start = (f32[32,80,128]{2,1,0:T(8,128)S(1)}, f32[32,80,128]{2,1,0:T(8,128)}, u32[]{:S(2)}) copy-start(f32[32,80,128]{2,1,0:T(8,128)} %shard_map.59.all_ref) | copy-start | bytes 3932164

commit v3 on v2

--- a/solution.py
+++ b/solution.py
@@ -236,44 +236,65 @@
 
 def solve_kernel(
     dims, place_ref, all_ref, forces_ref, left_ref,
-    search_a, search_b, image_a, image_b, rest_ref, info_ref, cos_ref, sin_ref, info_sem,
+    search_a, search_b, image_a, image_b, rest_ref,
+    index_vmem, normal_vmem, index_ref, normal_ref, table_sem,
 ):
     slabs, blocks, per_blocks, per_tiles, cases, lanes = dims
     chunks = all_ref.shape[0]
     disk_rows = 2 * cases
     cols = chunks // slabs
     base = per_blocks * disk_rows
-    listing = pltpu.make_async_copy(
-        all_ref.at[:, base + INFO_ROW : base + INFO_ROW + 1, :], info_ref, info_sem
-    )
-    listing.start()
+
+    words = all_ref[:, base + INFO_ROW, :].astype(jnp.int32)
+    after = pltpu.roll(words, lanes - 1, 1)
+    word = lax.broadcasted_iota(jnp.int32, words.shape, 1) & 3
+    piece_of = lax.broadcasted_iota(jnp.int32, words.shape, 0)
+    slab_of = jnp.zeros_like(words)
+    for s in range(1, slabs):
+        slab_of = slab_of + (piece_of >= s * cols).astype(jnp.int32)
+    upper_of = slab_of + after
+    upper_of = jnp.where(upper_of >= slabs, upper_of - slabs, upper_of)
+    index_vmem[...] = jnp.where(word == 0, slab_of, upper_of) * blocks + words
+    turn = jnp.where(word == 2, after, words)
+    normals = jnp.zeros(words.shape, jnp.float32)
     for k in range(6):
-        cos_ref[k] = COSINES[k]
-        sin_ref[k] = SINES[k]
-    listing.wait()
-
-    def apply_both(read_block, search_ref, image_ref):
-        image_ref[...] = jnp.zeros_like(image_ref)
+        normals = jnp.where(turn == k, jnp.where(word == 2, COSINES[k], SINES[k]), normals)
+    normal_vmem[...] = normals
+    image_a[...] = jnp.zeros_like(image_a)
+    image_b[...] = jnp.zeros_like(image_b)
+    tables = [
+        pltpu.make_async_copy(index_vmem, index_ref, table_sem.at[0]),
+        pltpu.make_async_copy(normal_vmem, normal_ref, table_sem.at[1]),
+    ]
+    for table in tables:
+        table.start()
+
+    def unpack(piece, carry):
+        for b in range(per_blocks):
+            rest_ref[piece * per_blocks + b] = all_ref[piece, b * disk_rows : (b + 1) * disk_rows, :]
+        return carry
+
+    lax.fori_loop(0, chunks, unpack, 0, unroll=4)
+    for table in tables:
+        table.wait()
+
+    def apply_both(search_ref, image_ref):
         sub = lax.broadcasted_iota(jnp.int32, (lanes, lanes), 0)
 
         def body(step, total):
             parts = []
             for u in range(UNROLL_CHUNKS):
                 piece = step * UNROLL_CHUNKS + u
-                slab = piece // cols
                 for k in range(per_tiles):
                     tile = piece * per_tiles + k
-                    info = [info_ref[piece, 0, 4 * k + w].astype(jnp.int32) for w in range(4)]
-                    first = slab * blocks + info[0]
-                    upper = lax.rem(slab + info[2], slabs)
-                    second = upper * blocks + info[1]
-                    turn = info[3]
-                    n0, n1 = cos_ref[turn], sin_ref[turn]
-                    spring = all_ref[piece, base + SPRING_ROW + k : base + SPRING_ROW + k + 1, :]
+                    first, second = index_ref[piece, 4 * k], index_ref[piece, 4 * k + 1]
+                    n0, n1 = normal_ref[piece, 4 * k + 2], normal_ref[piece, 4 * k + 3]
+                    at = base + SPRING_ROW + k
+                    spring = all_ref[piece, at : at + 1, :]
                     at = base + 2 * k
                     lane_i = all_ref[piece, at : at + 1, :].astype(jnp.int32)
                     lane_j = all_ref[piece, at + 1 : at + 2, :].astype(jnp.int32)
-                    vi, vj = read_block(first), read_block(second)
+                    vi, vj = rest_ref[first], rest_ref[second]
                     pi = n0 * vi[:cases] + n1 * vi[cases:]
                     pj = n0 * vj[:cases] + n1 * vj[cases:]
                     gi = jnp.take_along_axis(
@@ -315,10 +336,6 @@
         )
         return jnp.sum(total, axis=1, keepdims=True)
 
-    def chunk_rows(block):
-        start = pl.multiple_of(lax.rem(block, per_blocks) * disk_rows, 8)
-        return all_ref[block // per_blocks, pl.ds(start, disk_rows), :]
-
     def squares(field):
         both = jnp.sum(field * field, axis=0)
         return both[:cases] + both[cases:]
@@ -332,7 +349,7 @@
             keepdims=True,
         )
 
-    gamma = apply_both(chunk_rows, search_a, image_a)
+    gamma = apply_both(search_a, image_a)
 
     def norm_first(piece, total):
         return total + squares(image_a[pl.ds(piece * per_blocks, per_blocks)])
@@ -343,14 +360,11 @@
     def renew(piece, carry):
         for b in range(per_blocks):
             block = piece * per_blocks + b
-            rest_ref[block] = (
-                all_ref[piece, b * disk_rows : (b + 1) * disk_rows, :]
-                - alpha_rows * image_a[block]
-            )
+            rest_ref[block] = rest_ref[block] - alpha_rows * image_a[block]
         return carry
 
     lax.fori_loop(0, chunks, renew, 0, unroll=2)
-    gamma_next = apply_both(lambda block: rest_ref[block], search_b, image_b)
+    gamma_next = apply_both(search_b, image_b)
     beta = gamma_next / (gamma + EPS)
     beta_rows = jnp.concatenate([beta, beta], axis=0)
 
@@ -381,7 +395,7 @@
     smem = pl.BlockSpec(memory_space=pltpu.SMEM)
     everything = pl.pallas_call(
         functools.partial(gather_kernel, cols // SIDE, cols),
-        out_shape=jax.ShapeDtypeStruct((chunks, height, lanes), jnp.float32),
+        out_shape=pltpu.VMEM((chunks, height, lanes), jnp.float32),
         in_specs=[vmem] * 4,
         out_specs=vmem,
         scratch_shapes=[
@@ -408,13 +422,16 @@
             pltpu.VMEM(disk, jnp.float32),
             pltpu.VMEM(disk, jnp.float32),
             pltpu.VMEM(disk, jnp.float32),
-            pltpu.SMEM((chunks, 1, lanes), jnp.float32),
-            pltpu.SMEM((6,), jnp.float32),
-            pltpu.SMEM((6,), jnp.float32),
-            pltpu.SemaphoreType.DMA,
+            pltpu.VMEM((chunks, lanes), jnp.int32),
+            pltpu.VMEM((chunks, lanes), jnp.float32),
+            pltpu.SMEM((chunks, lanes), jnp.int32),
+            pltpu.SMEM((chunks, lanes), jnp.float32),
+            pltpu.SemaphoreType.DMA((2,)),
         ],
         compiler_params=pltpu.CompilerParams(vmem_limit_bytes=32 * 1024 * 1024),
-    )(place[None], everything)
+    )(
+        place[None], pltpu.with_memory_space_constraint(everything, pltpu.VMEM)
+    )
 
 
 def program_body(cols, rows, loads, stiffness, tile_info, offsets):

time: 36.6 us -> 33.1 us (0.904)
  Pallas kernels: 34.4 us -> 32.3 us
  local copies, waits for them, and re-layouts: 1.31 us -> 0 us
    unnamed x2 -> x0, local copies, waits for them, and re-layouts: 1.31 us -> none
    pallas_call x1, Pallas kernels: 20.9 us -> 19.8 us  [replicated(): pl.pallas_call(functools.partial(gather_kernel, cols // SIDE, cols), out_...]
    pallas_call x1, Pallas kernels: 13.5 us -> 12.5 us  [replicated(): pl.pallas_call(functools.partial(solve_kernel, dims), out_shape=(jax.Shap...]
where the time goes in v3:
time: 33.1 us; the launch traced here: 33 us
  Pallas kernels  32.3 us (98%)
  between operations  0.64 us (2%)
    pallas_call x1, Pallas kernels, replicated(): pl.pallas_call(functools.partial(gather_kernel, cols // SIDE, cols), out_...  19.8 us
    pallas_call x1, Pallas kernels, replicated(): pl.pallas_call(functools.partial(solve_kernel, dims), out_shape=(jax.Shap...  12.5 us

profile of v3, /device:TPU:0, one launch (start us, length us, event | category | flops | bytes accessed | tf_op | source)
XLA Modules:
  0.0 33.0 jit_solution(13376279699053094864)
XLA Ops:
  0.6 19.8 %shard_map.59.all_ref = f32[32,80,128]{2,1,0:T(8,128)S(1)} custom-call(f32[64,128]{1,0:T(8,128)} %bitcast.5, f32[4,128]{1,0:T(4,128)} %bitcast.7, s32[4,4]{1,0:T(4,128)} %bitcast.8, s32[8,128]{1,0:T(8,128)} %bitcast.6), custom_call_target="tpu_custom_call" | custom-call | tf_op jit(solution)/shard_map/pallas_call | solution.py:396
  20.5 12.5 %shard_map.60 = (f32[1,4,16,128]{3,2,1,0:T(8,128)}, f32[1,2,2,16,128]{4,3,2,1,0:T(8,128)}) custom-call(s32[1]{0:T(128)} %bitcast.place_ref, f32[32,80,128]{2,1,0:T(8,128)S(1)} %shard_map.59.all_ref), custom_call_target="tpu_custom_call" | custom-call | tf_op jit(solution)/shard_map/pallas_call | solution.py:411

commit v4 on v3

--- a/solution.py
+++ b/solution.py
@@ -237,7 +237,7 @@
 def solve_kernel(
     dims, place_ref, all_ref, forces_ref, left_ref,
     search_a, search_b, image_a, image_b, rest_ref,
-    index_vmem, normal_vmem, index_ref, normal_ref, table_sem,
+    pieces_ref, held_ref, index_vmem, normal_vmem, index_ref, normal_ref, table_sem,
 ):
     slabs, blocks, per_blocks, per_tiles, cases, lanes = dims
     chunks = all_ref.shape[0]
@@ -279,61 +279,79 @@
         table.wait()
 
     def apply_both(search_ref, image_ref):
-        sub = lax.broadcasted_iota(jnp.int32, (lanes, lanes), 0)
+        sub = lax.broadcasted_iota(jnp.int32, (lanes, lanes), 0).astype(jnp.float32).astype(jnp.bfloat16)
+        one, zero = jnp.bfloat16(1), jnp.bfloat16(0)
+
+        step_tiles = UNROLL_CHUNKS * per_tiles
+        held_ref[...] = jnp.zeros_like(held_ref)
+
+        def deposit_step(step):
+            for t in range(step_tiles):
+                piece, k = step * UNROLL_CHUNKS + t // per_tiles, t % per_tiles
+                first, second = index_ref[piece, 4 * k], index_ref[piece, 4 * k + 1]
+                n0, n1 = normal_ref[piece, 4 * k + 2], normal_ref[piece, 4 * k + 3]
+                one_end, other_end = held_ref[t, :, :lanes], held_ref[t, :, lanes:]
+                image_ref[first, :cases] += n0 * one_end
+                image_ref[first, cases:] += n1 * one_end
+                image_ref[second, :cases] -= n0 * other_end
+                image_ref[second, cases:] -= n1 * other_end
+
+        def prepare(step, total):
+            for t in range(step_tiles):
+                piece, k = step * UNROLL_CHUNKS + t // per_tiles, t % per_tiles
+                first, second = index_ref[piece, 4 * k], index_ref[piece, 4 * k + 1]
+                n0, n1 = normal_ref[piece, 4 * k + 2], normal_ref[piece, 4 * k + 3]
+                at = base + SPRING_ROW + k
+                spring = all_ref[piece, at : at + 1, :]
+                at = base + 2 * k
+                lane_i = all_ref[piece, at : at + 1, :].astype(jnp.int32)
+                lane_j = all_ref[piece, at + 1 : at + 2, :].astype(jnp.int32)
+                vi, vj = rest_ref[first], rest_ref[second]
+                pi = n0 * vi[:cases] + n1 * vi[cases:]
+                pj = n0 * vj[:cases] + n1 * vj[cases:]
+                gi = jnp.take_along_axis(
+                    pi, jnp.broadcast_to(lane_i, pi.shape), axis=1, mode="promise_in_bounds"
+                )
+                gj = jnp.take_along_axis(
+                    pj, jnp.broadcast_to(lane_j, pj.shape), axis=1, mode="promise_in_bounds"
+                )
+                value = spring * (gi - gj)
+                search_ref[piece * per_tiles + k] = value
+                total = total + value * value
+                weighted = spring * value
+                high = weighted.astype(jnp.bfloat16)
+                rest = weighted - high.astype(jnp.float32)
+                middle = rest.astype(jnp.bfloat16)
+                low = (rest - middle.astype(jnp.float32)).astype(jnp.bfloat16)
+                pieces_ref[t] = jnp.concatenate([high, middle, low], axis=0)
+            return total
+
+        def products(step):
+            for t in range(step_tiles):
+                piece, k = step * UNROLL_CHUNKS + t // per_tiles, t % per_tiles
+                at = base + 2 * k
+                spot_i = all_ref[piece, at : at + 1, :].astype(jnp.bfloat16)
+                spot_j = all_ref[piece, at + 1 : at + 2, :].astype(jnp.bfloat16)
+                hot = jnp.concatenate(
+                    [jnp.where(sub == spot_i, one, zero), jnp.where(sub == spot_j, one, zero)],
+                    axis=0,
+                )
+                out = lax.dot_general(
+                    pieces_ref[t], hot, (((1,), (1,)), ((), ())), preferred_element_type=jnp.float32
+                )
+                held_ref[t] = out[:cases] + (out[cases : 2 * cases] + out[2 * cases :])
 
         def body(step, total):
-            parts = []
-            for u in range(UNROLL_CHUNKS):
-                piece = step * UNROLL_CHUNKS + u
-                for k in range(per_tiles):
-                    tile = piece * per_tiles + k
-                    first, second = index_ref[piece, 4 * k], index_ref[piece, 4 * k + 1]
-                    n0, n1 = normal_ref[piece, 4 * k + 2], normal_ref[piece, 4 * k + 3]
-                    at = base + SPRING_ROW + k
-                    spring = all_ref[piece, at : at + 1, :]
-                    at = base + 2 * k
-                    lane_i = all_ref[piece, at : at + 1, :].astype(jnp.int32)
-                    lane_j = all_ref[piece, at + 1 : at + 2, :].astype(jnp.int32)
-                    vi, vj = rest_ref[first], rest_ref[second]
-                    pi = n0 * vi[:cases] + n1 * vi[cases:]
-                    pj = n0 * vj[:cases] + n1 * vj[cases:]
-                    gi = jnp.take_along_axis(
-                        pi, jnp.broadcast_to(lane_i, pi.shape), axis=1, mode="promise_in_bounds"
-                    )
-                    gj = jnp.take_along_axis(
-                        pj, jnp.broadcast_to(lane_j, pj.shape), axis=1, mode="promise_in_bounds"
-                    )
-                    value = spring * (gi - gj)
-                    search_ref[tile] = value
-                    total = total + value * value
-                    weighted = spring * value
-                    high = weighted.astype(jnp.bfloat16)
-                    rest = weighted - high.astype(jnp.float32)
-                    middle = rest.astype(jnp.bfloat16)
-                    low = (rest - middle.astype(jnp.float32)).astype(jnp.bfloat16)
-                    lhs = jnp.concatenate([high, middle, low], axis=0)
-                    hot = jnp.concatenate(
-                        [
-                            jnp.where(sub == lane_i, 1.0, 0.0).astype(jnp.bfloat16),
-                            jnp.where(sub == lane_j, 1.0, 0.0).astype(jnp.bfloat16),
-                        ],
-                        axis=0,
-                    )
-                    out = lax.dot_general(
-                        lhs, hot, (((1,), (1,)), ((), ())), preferred_element_type=jnp.float32
-                    )
-                    out = out[:cases] + (out[cases : 2 * cases] + out[2 * cases :])
-                    parts.append((first, second, n0, n1, out[:, :lanes], out[:, lanes:]))
-            for first, second, n0, n1, one, two in parts:
-                image_ref[first, :cases] += n0 * one
-                image_ref[first, cases:] += n1 * one
-                image_ref[second, :cases] -= n0 * two
-                image_ref[second, cases:] -= n1 * two
-            return total
-
-        total = lax.fori_loop(
-            0, chunks // UNROLL_CHUNKS, body, jnp.zeros((cases, lanes), jnp.float32)
-        )
+            deposit_step(jnp.maximum(step - 1, 0))
+            products(step)
+            return prepare(step + 1, total)
+
+        steps = chunks // UNROLL_CHUNKS
+        total = prepare(0, jnp.zeros((cases, lanes), jnp.float32))
+        total = lax.fori_loop(0, steps - 1, body, total)
+        deposit_step(steps - 2)
+        products(steps - 1)
+        deposit_step(steps - 1)
         return jnp.sum(total, axis=1, keepdims=True)
 
     def squares(field):
@@ -422,6 +440,8 @@
             pltpu.VMEM(disk, jnp.float32),
             pltpu.VMEM(disk, jnp.float32),
             pltpu.VMEM(disk, jnp.float32),
+            pltpu.VMEM((UNROLL_CHUNKS * per_tiles, 3 * cases, lanes), jnp.bfloat16),
+            pltpu.VMEM((UNROLL_CHUNKS * per_tiles, cases, 2 * lanes), jnp.float32),
             pltpu.VMEM((chunks, lanes), jnp.int32),
             pltpu.VMEM((chunks, lanes), jnp.float32),
             pltpu.SMEM((chunks, lanes), jnp.int32),

time: 33.1 us -> 33.2 us (level)
  no operation moved by 1% of the time
where the time goes in v4:
time: 33.2 us; the launch traced here: 33 us
  Pallas kernels  32.4 us (98%)
  between operations  0.64 us (2%)
    pallas_call x1, Pallas kernels, replicated(): pl.pallas_call(functools.partial(gather_kernel, cols // SIDE, cols), out_...  19.8 us
    pallas_call x1, Pallas kernels, replicated(): pl.pallas_call(functools.partial(solve_kernel, dims), out_shape=(jax.Shap...  12.6 us

profile of v4, /device:TPU:0, one launch (start us, length us, event | category | flops | bytes accessed | tf_op | source)
XLA Modules:
  0.0 33.0 jit_solution(4778585287099806375)
XLA Ops:
  0.6 19.8 %shard_map.59.all_ref = f32[32,80,128]{2,1,0:T(8,128)S(1)} custom-call(f32[64,128]{1,0:T(8,128)} %bitcast.5, f32[4,128]{1,0:T(4,128)} %bitcast.7, s32[4,4]{1,0:T(4,128)} %bitcast.8, s32[8,128]{1,0:T(8,128)} %bitcast.6), custom_call_target="tpu_custom_call" | custom-call | tf_op jit(solution)/shard_map/pallas_call | solution.py:414
  20.5 12.6 %shard_map.60 = (f32[1,4,16,128]{3,2,1,0:T(8,128)}, f32[1,2,2,16,128]{4,3,2,1,0:T(8,128)}) custom-call(s32[1]{0:T(128)} %bitcast.place_ref, f32[32,80,128]{2,1,0:T(8,128)S(1)} %shard_map.59.all_ref), custom_call_target="tpu_custom_call" | custom-call | tf_op jit(solution)/shard_map/pallas_call | solution.py:429
